TPU v7x, 32 devices: a whole 2x2x4 slice. The times are simulated.
32 devices in a mesh: dp: 4 (over x, core), ctx: 8 (over z, y).
Axes of the slice: x: 2, y: 2, z: 4, core: 2. Of those that a mesh axis runs over, the one named last changes fastest.
Arguments:
- query: bfloat16 [4, 1024, 2048], P('dp', 'ctx'), may hold values from -6 to 6
- keys: bfloat16 [4, 1024, 2048], P('dp', 'ctx'), may hold values from -6 to 6
- values: bfloat16 [4, 1024, 2048], P('dp', 'ctx'), may hold values from -6 to 6
- cotangent: bfloat16 [4, 1024, 2048], P('dp', 'ctx'), may hold values from -6 to 6
- long_filter: bfloat16 [1024, 2048], P('ctx'), may hold values from -1.05 to 1.05, as said below
- short_weights: float32 [3, 3, 2048], replicated, may hold values from -3 to 3
- skip: float32 [2048], replicated, may hold values from -4 to 4
- lengths: int32 [4, 16], P('dp'), may hold values from 1 to 256, 1024 in all within a row
Outputs:
- gated: bfloat16 [4, 1024, 2048], P('dp', 'ctx')
- grad_query: bfloat16 [4, 1024, 2048], P('dp', 'ctx')
- grad_keys: bfloat16 [4, 1024, 2048], P('dp', 'ctx')
- grad_values: bfloat16 [4, 1024, 2048], P('dp', 'ctx')
- grad_filter: float32 [1024, 2048], P('ctx', 'dp')
- grad_short: float32 [3, 3, 2048], replicated
- grad_skip: float32 [2048], replicated
Inputs may be any that keep to these rules, and one draw needn't show every extreme that they name: Each row lists, in order, the lengths of the 16 documents packed into one sequence; they sum to 1024 and the longest is exactly 256. `long_filter`: one filter for every channel over the lags 0 .. 1023.
All inputs are finite; a program needn't handle non-finite values.
Results may differ from a plain program's by a relative error of at most 0.024.
Values may be sent and summed in bfloat16 or wider, within the bound.
No kernel may reach another device: no remote copies, remote signals or barrier semaphores. Data moves between devices by JAX's collectives and lax.ppermute only.
A program may use at most 192 MiB of HBM per device.

v0:
```python
import jax
import jax.numpy as jnp
from jax import lax
from jax.sharding import PartitionSpec as P


def shifted(x, axis, by):
    length = lax.axis_size(axis)
    pairs = [(i, i + by) for i in range(length) if 0 <= i + by < length]
    return lax.ppermute(x, axis, pairs)


def angles(time_idx, freq_idx, modulus, twist):
    turns = 2 * (time_idx * freq_idx % modulus) - twist * time_idx
    return jnp.pi * turns.astype(jnp.float32) / modulus


def table_halves(table):
    upper = lax.optimization_barrier(table.astype(jnp.bfloat16))
    lower = (table - upper.astype(jnp.float32)).astype(jnp.bfloat16)
    return (upper, lower)


def split_product(form, table, data):
    upper, lower = table_halves(table)
    if data.dtype == jnp.bfloat16:
        total = jnp.einsum(form, upper, data, preferred_element_type=jnp.float32)
        return total + jnp.einsum(form, lower, data, preferred_element_type=jnp.float32)
    data_upper = lax.optimization_barrier(data.astype(jnp.bfloat16))
    data_lower = (data - data_upper.astype(jnp.float32)).astype(jnp.bfloat16)
    total = jnp.einsum(form, upper, data_upper, preferred_element_type=jnp.float32)
    total = total + jnp.einsum(form, lower, data_upper, preferred_element_type=jnp.float32)
    return total + jnp.einsum(form, upper, data_lower, preferred_element_type=jnp.float32)


def dft_block(rows, direction):
    steps = jnp.arange(rows, dtype=jnp.int32)
    phase = angles(steps[:, None], steps[None, :], rows, 0)
    cosine = jnp.cos(phase)
    sine = direction * jnp.sin(phase)
    upper = jnp.concatenate([cosine, sine], 1)
    lower = jnp.concatenate([-sine, cosine], 1)
    return jnp.concatenate([upper, lower], 0)


def to_columns(data):
    return lax.all_to_all(data, "ctx", split_axis=0, concat_axis=0, tiled=True)


def to_rows(data):
    return lax.all_to_all(data, "ctx", split_axis=0, concat_axis=0, tiled=True)


def forward_spectrum(columns, index):
    parts, block, chans = columns.shape
    rows = parts * block
    seq_len = rows * parts
    time_p = jnp.arange(parts, dtype=jnp.int32)[None, :]
    freq_k = jnp.arange(parts, dtype=jnp.int32)[:, None]
    tables = []
    for twist in range(2):
        phase = angles(time_p, freq_k, parts, twist)
        tables.append(jnp.cos(phase))
        tables.append(-jnp.sin(phase))
    table = jnp.stack(tables).reshape(4 * parts, parts)
    flat = columns.reshape(parts, block * chans)
    partial_value = split_product("kp,pm->km", table, flat)
    partial_value = partial_value.reshape(2, 2, parts, block, chans)
    local_m = index * block + jnp.arange(block, dtype=jnp.int32)
    twiddled = []
    for twist in range(2):
        phase = angles(local_m[None, :], freq_k, seq_len, twist)[:, :, None]
        cosine = jnp.cos(phase)
        sine = jnp.sin(phase)
        real_part = partial_value[twist, 0]
        imag_part = partial_value[twist, 1]
        twiddled.append(real_part * cosine + imag_part * sine)
        twiddled.append(imag_part * cosine - real_part * sine)
    moved = lax.all_to_all(jnp.stack(twiddled), "ctx", split_axis=1, concat_axis=2, tiled=True)
    data = moved.reshape(2, 2 * rows, chans)
    spectrum = split_product("ab,sbc->sac", dft_block(rows, 1.0), data)
    return spectrum.reshape(2, 2, rows, chans)


def inverse_spectrum(spectrum, index, parts):
    rows, chans = (spectrum.shape[2], spectrum.shape[3])
    block = rows // parts
    seq_len = rows * parts
    data = spectrum.reshape(2, 2 * rows, chans)
    back = split_product("ab,sbc->sac", dft_block(rows, -1.0), data).reshape(2, 2, rows, chans)
    local_m = jnp.arange(rows, dtype=jnp.int32)[:, None]
    twisted = []
    for twist in range(2):
        phase = angles(local_m, index, seq_len, twist)
        cosine = jnp.cos(phase)
        sine = jnp.sin(phase)
        real_part = back[twist, 0]
        imag_part = back[twist, 1]
        twisted.append(real_part * cosine - imag_part * sine)
        twisted.append(imag_part * cosine + real_part * sine)
    stacked = jnp.stack(twisted).reshape(4, parts, block, chans)
    moved = (
        lax.all_to_all(stacked.astype(jnp.bfloat16), "ctx", split_axis=1, concat_axis=2, tiled=True)
        .astype(stacked.dtype)
        .reshape(4 * parts, block * chans)
    )
    time_p = jnp.arange(parts, dtype=jnp.int32)[:, None]
    freq_k = jnp.arange(parts, dtype=jnp.int32)[None, :]
    pieces = []
    for twist in range(2):
        phase = angles(time_p, freq_k, parts, twist)
        pieces.append(jnp.cos(phase))
        pieces.append(-jnp.sin(phase))
    table = jnp.stack(pieces, axis=1).reshape(parts, 4 * parts) / (2.0 * seq_len)
    result = split_product("kp,pm->km", table, moved)
    return result.reshape(parts, block, chans)


def spectrum_of(signal, index, parts):
    rows, channels = signal.shape
    columns = to_columns(signal).reshape(parts, rows // parts, channels)
    return forward_spectrum(columns, index)


def signal_of(spectrum, index, parts):
    rows, channels = (spectrum.shape[2], spectrum.shape[3])
    return to_rows(inverse_spectrum(spectrum, index, parts).reshape(rows, channels))


def complex_product(left_re, left_im, right_re, right_im, conjugate_left):
    if conjugate_left:
        return (left_re * right_re + left_im * right_im, left_re * right_im - left_im * right_re)
    return (left_re * right_re - left_im * right_im, left_re * right_im + left_im * right_re)


def spectral_product(first, second, conjugate_left):
    twists = []
    for twist in range(2):
        twists.append(
            jnp.stack(
                complex_product(
                    first[twist, 0],
                    first[twist, 1],
                    second[twist, 0],
                    second[twist, 1],
                    conjugate_left,
                )
            )
        )
    return jnp.stack(twists)


def short_forward(padded, weights, valid):
    count = weights.shape[0]
    rows = padded.shape[0] - count + 1
    wide = padded.astype(jnp.float32)
    summed = weights[0] * wide[count - 1 :]
    for offset in range(1, count):
        begin = count - 1 - offset
        summed = summed + jnp.where(
            valid[offset][:, None], weights[offset] * wide[begin : begin + rows], 0.0
        )
    return summed


def short_backward(padded, grad_short, after, weights, valid, valid_after):
    count = weights.shape[0]
    rows = grad_short.shape[0]
    wide = padded.astype(jnp.float32)
    extended = jnp.concatenate([grad_short, after], 0)
    grad_source = weights[0] * grad_short
    weight_grads = [jnp.sum(wide[count - 1 :] * grad_short, axis=0)]
    for offset in range(1, count):
        later = jnp.where(
            valid_after[offset, offset : offset + rows][:, None],
            extended[offset : offset + rows],
            0.0,
        )
        grad_source = grad_source + weights[offset] * later
        masked = jnp.where(valid[offset][:, None], grad_short, 0.0)
        begin = count - 1 - offset
        weight_grads.append(jnp.sum(masked * wide[begin : begin + rows], axis=0))
    return (grad_source, jnp.stack(weight_grads))


def local(query, keys, values, cotangent, long_filter, short_weights, skip, lengths):
    parts = lax.axis_size("ctx")
    index = lax.axis_index("ctx")
    groups = lax.axis_size("dp")
    q_rows = query[0]
    k_rows = keys[0]
    v_rows = values[0]
    upstream = cotangent[0].astype(jnp.float32)
    rows, chans = q_rows.shape
    taps = short_weights.shape[1]
    seq_len = rows * parts
    doc_len = lengths[0]
    starts = jnp.cumsum(doc_len) - doc_len

    def valid_mask(where):
        begin = jnp.max(jnp.where(starts[None, :] <= where[:, None], starts[None, :], 0), axis=1)
        shifts = jnp.arange(taps, dtype=jnp.int32)[:, None]
        return where[None, :] - shifts >= begin[None, :]

    position = index * rows + jnp.arange(rows, dtype=jnp.int32)
    valid = valid_mask(position)
    valid_after = valid_mask(index * rows + jnp.arange(rows + taps - 1, dtype=jnp.int32))
    edge = rows - taps + 1
    rim = shifted((q_rows[edge:], k_rows[edge:], v_rows[edge:]), "ctx", 1)
    padded_q = jnp.concatenate([rim[0], q_rows], 0)
    padded_k = jnp.concatenate([rim[1], k_rows], 0)
    padded_v = jnp.concatenate([rim[2], v_rows], 0)
    q_short = (
        short_forward(padded_q, short_weights[0], valid).astype(jnp.bfloat16).astype(jnp.float32)
    )
    k_short = (
        short_forward(padded_k, short_weights[1], valid).astype(jnp.bfloat16).astype(jnp.float32)
    )
    v_short = (
        short_forward(padded_v, short_weights[2], valid).astype(jnp.bfloat16).astype(jnp.float32)
    )
    mixed = (k_short * v_short).astype(jnp.bfloat16)
    grad_conv = (upstream * q_short).astype(jnp.bfloat16)
    mixed_wide = mixed.astype(jnp.float32)
    grad_wide = grad_conv.astype(jnp.float32)
    spectrum_f = spectrum_of(long_filter, index, parts)
    spectrum_x = spectrum_of(mixed, index, parts)
    spectrum_g = spectrum_of(grad_conv, index, parts)
    conv_spec = spectral_product(spectrum_x, spectrum_f, False)
    back_spec = spectral_product(spectrum_f, spectrum_g, True)
    cross_spec = spectral_product(spectrum_x, spectrum_g, True)
    conv_raw = signal_of(conv_spec, index, parts)
    back_raw = signal_of(back_spec, index, parts)
    lagged = signal_of(cross_spec, index, parts)
    filter_part = lax.psum_scatter(
        lagged.astype(jnp.bfloat16), "dp", scatter_dimension=1, tiled=True
    ).astype(jnp.float32)
    conv = conv_raw + skip * mixed_wide
    gated = (q_short * conv).astype(jnp.bfloat16)
    grad_qs = upstream * conv
    grad_mixed = back_raw + skip * grad_wide
    grad_ks = grad_mixed * v_short
    grad_vs = grad_mixed * k_short
    skip_grad = jnp.sum(grad_wide * mixed_wide, axis=0)
    head = taps - 1
    after = shifted((grad_qs[:head], grad_ks[:head], grad_vs[:head]), "ctx", -1)
    grad_q, short_q = short_backward(
        padded_q, grad_qs, after[0], short_weights[0], valid, valid_after
    )
    grad_k, short_k = short_backward(
        padded_k, grad_ks, after[1], short_weights[1], valid, valid_after
    )
    grad_v, short_v = short_backward(
        padded_v, grad_vs, after[2], short_weights[2], valid, valid_after
    )
    summed = lax.psum((jnp.stack([short_q, short_k, short_v]), skip_grad), ("dp", "ctx"))
    scale = 1.0 / (groups * seq_len)
    return (
        gated[None],
        grad_q.astype(jnp.bfloat16)[None],
        grad_k.astype(jnp.bfloat16)[None],
        grad_v.astype(jnp.bfloat16)[None],
        filter_part * scale,
        summed[0] * scale,
        summed[1] * scale,
    )


def solution(mesh):
    in_specs = (
        P("dp", "ctx", None),
        P("dp", "ctx", None),
        P("dp", "ctx", None),
        P("dp", "ctx", None),
        P("ctx", None),
        P(),
        P(),
        P("dp", None),
    )
    out_specs = (
        P("dp", "ctx", None),
        P("dp", "ctx", None),
        P("dp", "ctx", None),
        P("dp", "ctx", None),
        P("ctx", "dp"),
        P(),
        P(),
    )
    return jax.shard_map(local, mesh=mesh, in_specs=in_specs, out_specs=out_specs, check_vma=False)
```

profile of v0, /device:TPU:0, one launch (start us, length us, event | category | flops | bytes accessed | tf_op | source)
XLA Modules:
  0.0 839.0 jit_solution(11256855569213254024)
XLA Ops:
  8.8 4.9 collective-permute-start
  22.2 4.0 all-to-all-start.2
  46.8 10.4 %all-to-all-done = bf16[8,16,2048]{2,1,0:T(8,128)(2,1)S(1)} async-done(((bf16[8,16,2048]{2,1,0:T(8,128)(2,1)}), bf16[8,16,2048]{2,1,0:T(8,128)(2,1)S(1)}, u32[]{:S(2)}, u32[]{:S(2)}) %all-to-all-start) | async-done | bytes 524320 | tf_op jit(solution)/shard_map/all_to_all | solution.py:47
  64.8 9.9 %all-to-all-done.6 = bf16[8,16,2048]{2,1,0:T(8,128)(2,1)S(1)} async-done(((bf16[8,16,2048]{2,1,0:T(8,128)(2,1)}), bf16[8,16,2048]{2,1,0:T(8,128)(2,1)S(1)}, u32[]{:S(2)}, u32[]{:S(2)}) %all-to-all-start.6) | async-done | bytes 524320 | tf_op jit(solution)/shard_map/all_to_all | solution.py:47
  78.5 5.5 multiply_add_fusion.1
  84.1 6.2 multiply_add_fusion
  92.6 4.7 all-to-all-start.3
  97.3 4.0 pad_maximum_fusion
  101.3 87.9 %all-to-all-done.3 = f32[4,8,16,2048]{3,2,0,1:T(8,128)} async-done(((f32[4,8,16,2048]{3,2,0,1:T(8,128)}), f32[4,8,16,2048]{3,2,0,1:T(8,128)}, u32[]{:S(2)}, u32[]{:S(2)}) %all-to-all-start.3) | async-done | bytes 4194336 | tf_op jit(solution)/shard_map/all_to_all | solution.py:79
  189.2 4.6 all-to-all-start.1
  197.4 89.0 %all-to-all-done.1 = f32[4,8,16,2048]{3,2,0,1:T(8,128)} async-done(((f32[4,8,16,2048]{3,2,0,1:T(8,128)}), f32[4,8,16,2048]{3,2,0,1:T(8,128)}, u32[]{:S(2)}, u32[]{:S(2)}) %all-to-all-start.1) | async-done | bytes 4194336 | tf_op jit(solution)/shard_map/all_to_all | solution.py:79
  286.3 4.6 all-to-all-start.7
  313.1 70.3 %all-to-all-done.7 = f32[4,8,16,2048]{3,2,0,1:T(8,128)} async-done(((f32[4,8,16,2048]{3,2,0,1:T(8,128)}), f32[4,8,16,2048]{3,2,0,1:T(8,128)}, u32[]{:S(2)}, u32[]{:S(2)}) %all-to-all-start.7) | async-done | bytes 4194336 | tf_op jit(solution)/shard_map/all_to_all | solution.py:79
  397.0 4.6 add_add_fusion.5
  407.2 4.8 add_add_fusion.2
  446.5 4.0 all-to-all-start.4
  453.3 45.6 %all-to-all-done.4 = bf16[4,8,16,2048]{3,2,0,1:T(8,128)(2,1)S(1)} async-done(((bf16[4,8,16,2048]{3,2,0,1:T(8,128)(2,1)}), bf16[4,8,16,2048]{3,2,0,1:T(8,128)(2,1)S(1)}, u32[]{:S(2)}, u32[]{:S(2)}) %all-to-all-start.4) | async-done | bytes 2097184 | tf_op jit(solution)/shard_map/all_to_all | solution.py:103
  506.7 45.6 %all-to-all-done.8 = bf16[4,8,16,2048]{3,2,0,1:T(8,128)(2,1)S(1)} async-done(((bf16[4,8,16,2048]{3,2,0,1:T(8,128)(2,1)}), bf16[4,8,16,2048]{3,2,0,1:T(8,128)(2,1)S(1)}, u32[]{:S(2)}, u32[]{:S(2)}) %all-to-all-start.8) | async-done | bytes 2097184 | tf_op jit(solution)/shard_map/all_to_all | solution.py:103
  563.3 42.4 %all-to-all-done.10 = bf16[4,8,16,2048]{3,2,0,1:T(8,128)(2,1)S(1)} async-done(((bf16[4,8,16,2048]{3,2,0,1:T(8,128)(2,1)}), bf16[4,8,16,2048]{3,2,0,1:T(8,128)(2,1)S(1)}, u32[]{:S(2)}, u32[]{:S(2)}) %all-to-all-start.10) | async-done | bytes 2097184 | tf_op jit(solution)/shard_map/all_to_all | solution.py:103
  615.2 20.1 %all-to-all-done.5 = f32[8,16,2048]{2,1,0:T(8,128)S(1)} async-done(((f32[8,16,2048]{2,1,0:T(8,128)}), f32[8,16,2048]{2,1,0:T(8,128)S(1)}, u32[]{:S(2)}, u32[]{:S(2)}) %all-to-all-start.5) | async-done | bytes 1048608 | tf_op jit(solution)/shard_map/all_to_all | solution.py:51
  640.1 46.0 %psum.15 = f32[2048]{0:T(1024)S(1)} all-reduce(f32[2048]{0:T(1024)S(1)} %copy-done.61), channel_id=1, replica_groups=mesh['dp'=4,'ctx'=8] {'dp','ctx'}, use_global_device_ids=true, to_apply=%region_15.16 | all-reduce | flops 2048 | bytes 16384 | tf_op jit(solution)/shard_map/psum | solution.py:256
  693.4 5.3 all-to-all-start.11
  706.3 5.6 all-to-all-done.11
  722.4 105.7 %all-reduce.2.cloned.1.call-done = f32[3,3,2048]{2,1,0:T(4,128)} async-done(((f32[3,3,2048]{2,1,0:T(4,128)}), f32[3,3,2048]{2,1,0:T(4,128)}) %all-reduce.2.cloned.1.call-update) | async-done | bytes 73744 | tf_op jit(solution)/shard_map/psum | solution.py:256
  (288 shorter events, 186.5 us)
Async XLA Ops:
  8.8 20.9 %collective-permute-start = (bf16[2,2048]{1,0:T(2,128)(2,1)S(1)}, bf16[2,2048]{1,0:T(2,128)(2,1)S(1)}, u32[]{:S(2)}, u32[]{:S(2)}) collective-permute-start(bf16[2,2048]{1,0:T(2,128)(2,1)S(1)} %slice_bitcast_fusion.2), channel_id=1, source_target_pairs={{0,1},{1,2},{2,3},{3,4},{4,5},{5,6},{6,7},{8,9},{9,10},{10,11},{11... | collective-permute-start | bytes 24584 | tf_op jit(solution)/shard_map/ppermute | solution.py:10
  14.5 16.5 %collective-permute-start.1 = (bf16[2,2048]{1,0:T(2,128)(2,1)S(1)}, bf16[2,2048]{1,0:T(2,128)(2,1)S(1)}, u32[]{:S(2)}, u32[]{:S(2)}) collective-permute-start(bf16[2,2048]{1,0:T(2,128)(2,1)S(1)} %slice_bitcast_fusion.1), channel_id=1, source_target_pairs={{0,1},{1,2},{2,3},{3,4},{4,5},{5,6},{6,7},{8,9},{9,10},{10,11},{11... | collective-permute-start | bytes 24584 | tf_op jit(solution)/shard_map/ppermute | solution.py:10
  18.7 12.5 %collective-permute-start.2 = (bf16[2,2048]{1,0:T(2,128)(2,1)S(1)}, bf16[2,2048]{1,0:T(2,128)(2,1)S(1)}, u32[]{:S(2)}, u32[]{:S(2)}) collective-permute-start(bf16[2,2048]{1,0:T(2,128)(2,1)S(1)} %slice_bitcast_fusion), channel_id=1, source_target_pairs={{0,1},{1,2},{2,3},{3,4},{4,5},{5,6},{6,7},{8,9},{9,10},{10,11},{11... | collective-permute-start | bytes 24584 | tf_op jit(solution)/shard_map/ppermute | solution.py:10
  22.2 17.7 %all-to-all-start.2 = ((bf16[8,16,2048]{2,1,0:T(8,128)(2,1)}), bf16[8,16,2048]{2,1,0:T(8,128)(2,1)S(1)}, u32[]{:S(2)}, u32[]{:S(2)}) async-start(bf16[8,16,2048]{2,1,0:T(8,128)(2,1)} %bitcast.384), calls=%async_computation.2 | async-start | bytes 1048576 | tf_op jit(solution)/shard_map/all_to_all | solution.py:47
  39.9 17.4 %all-to-all-start = ((bf16[8,16,2048]{2,1,0:T(8,128)(2,1)}), bf16[8,16,2048]{2,1,0:T(8,128)(2,1)S(1)}, u32[]{:S(2)}, u32[]{:S(2)}) async-start(bf16[8,16,2048]{2,1,0:T(8,128)(2,1)} %bitcast.19), calls=%async_computation | async-start | bytes 1048576 | tf_op jit(solution)/shard_map/all_to_all | solution.py:47
  57.3 17.4 %all-to-all-start.6 = ((bf16[8,16,2048]{2,1,0:T(8,128)(2,1)}), bf16[8,16,2048]{2,1,0:T(8,128)(2,1)S(1)}, u32[]{:S(2)}, u32[]{:S(2)}) async-start(bf16[8,16,2048]{2,1,0:T(8,128)(2,1)} %bitcast.64), calls=%async_computation.6 | async-start | bytes 1048576 | tf_op jit(solution)/shard_map/all_to_all | solution.py:47
  92.6 96.6 %all-to-all-start.3 = ((f32[4,8,16,2048]{3,2,0,1:T(8,128)}), f32[4,8,16,2048]{3,2,0,1:T(8,128)}, u32[]{:S(2)}, u32[]{:S(2)}) async-start(f32[4,8,16,2048]{3,2,0,1:T(8,128)} %pad_maximum_fusion.1), calls=%async_computation.3 | async-start | bytes 8388608 | tf_op jit(solution)/shard_map/all_to_all | solution.py:79
  101.3 92.5 %copy-start.23 = (f32[1,8,16,2048]{3,2,0,1:T(8,128)S(1)}, f32[1,8,16,2048]{3,2,0,1:T(8,128)}, u32[]{:S(2)}) copy-start(f32[1,8,16,2048]{3,2,0,1:T(8,128)} %get-tuple-element.70) | copy-start | bytes 3145732
  101.3 92.5 %copy-start.31 = (f32[1,8,16,2048]{3,2,0,1:T(8,128)S(1)}, f32[1,8,16,2048]{3,2,0,1:T(8,128)}, u32[]{:S(2)}) copy-start(f32[1,8,16,2048]{3,2,0,1:T(8,128)} %get-tuple-element.71) | copy-start | bytes 3145732
  189.2 97.1 %all-to-all-start.1 = ((f32[4,8,16,2048]{3,2,0,1:T(8,128)}), f32[4,8,16,2048]{3,2,0,1:T(8,128)}, u32[]{:S(2)}, u32[]{:S(2)}) async-start(f32[4,8,16,2048]{3,2,0,1:T(8,128)} %pad_maximum_fusion), calls=%async_computation.1 | async-start | bytes 8388608 | tf_op jit(solution)/shard_map/all_to_all | solution.py:79
  286.3 97.1 %all-to-all-start.7 = ((f32[4,8,16,2048]{3,2,0,1:T(8,128)}), f32[4,8,16,2048]{3,2,0,1:T(8,128)}, u32[]{:S(2)}, u32[]{:S(2)}) async-start(f32[4,8,16,2048]{3,2,0,1:T(8,128)} %pad_maximum_fusion.3), calls=%async_computation.7 | async-start | bytes 8388608 | tf_op jit(solution)/shard_map/all_to_all | solution.py:79
  446.5 52.4 %all-to-all-start.4 = ((bf16[4,8,16,2048]{3,2,0,1:T(8,128)(2,1)}), bf16[4,8,16,2048]{3,2,0,1:T(8,128)(2,1)S(1)}, u32[]{:S(2)}, u32[]{:S(2)}) async-start(bf16[4,8,16,2048]{3,2,0,1:T(8,128)(2,1)} %pad_maximum_fusion.8), calls=%async_computation.4 | async-start | bytes 4194304 | tf_op jit(solution)/shard_map/all_to_all | solution.py:103
  453.3 50.6 %copy-start.37 = (bf16[1,8,16,2048]{3,2,0,1:T(8,128)(2,1)S(1)}, bf16[1,8,16,2048]{3,2,0,1:T(8,128)(2,1)}, u32[]{:S(2)}) copy-start(bf16[1,8,16,2048]{3,2,0,1:T(8,128)(2,1)} %get-tuple-element.61) | copy-start | bytes 1572868
  453.3 50.6 %copy-start.38 = (bf16[1,8,16,2048]{3,2,0,1:T(8,128)(2,1)S(1)}, bf16[1,8,16,2048]{3,2,0,1:T(8,128)(2,1)}, u32[]{:S(2)}) copy-start(bf16[1,8,16,2048]{3,2,0,1:T(8,128)(2,1)} %get-tuple-element.62) | copy-start | bytes 1572868
  500.3 52.1 %all-to-all-start.8 = ((bf16[4,8,16,2048]{3,2,0,1:T(8,128)(2,1)}), bf16[4,8,16,2048]{3,2,0,1:T(8,128)(2,1)S(1)}, u32[]{:S(2)}, u32[]{:S(2)}) async-start(bf16[4,8,16,2048]{3,2,0,1:T(8,128)(2,1)} %pad_maximum_fusion.11), calls=%async_computation.8 | async-start | bytes 4194304 | tf_op jit(solution)/shard_map/all_to_all | solution.py:103
  553.6 52.1 %all-to-all-start.10 = ((bf16[4,8,16,2048]{3,2,0,1:T(8,128)(2,1)}), bf16[4,8,16,2048]{3,2,0,1:T(8,128)(2,1)S(1)}, u32[]{:S(2)}, u32[]{:S(2)}) async-start(bf16[4,8,16,2048]{3,2,0,1:T(8,128)(2,1)} %pad_maximum_fusion.14), calls=%async_computation.10 | async-start | bytes 4194304 | tf_op jit(solution)/shard_map/all_to_all | solution.py:103
  605.7 29.6 %all-to-all-start.5 = ((f32[8,16,2048]{2,1,0:T(8,128)}), f32[8,16,2048]{2,1,0:T(8,128)S(1)}, u32[]{:S(2)}, u32[]{:S(2)}) async-start(f32[8,16,2048]{2,1,0:T(8,128)} %copy.115), calls=%async_computation.5 | async-start | bytes 2097152 | tf_op jit(solution)/shard_map/all_to_all | solution.py:51
  636.3 57.1 %all-to-all-start.9 = ((f32[8,16,2048]{2,1,0:T(8,128)}), f32[8,16,2048]{2,1,0:T(8,128)S(1)}, u32[]{:S(2)}, u32[]{:S(2)}) async-start(f32[8,16,2048]{2,1,0:T(8,128)} %copy.122), calls=%async_computation.9 | async-start | bytes 2097152 | tf_op jit(solution)/shard_map/all_to_all | solution.py:51
  693.4 18.5 %all-to-all-start.11 = ((bf16[8,16,2048]{2,1,0:T(8,128)(2,1)}), bf16[8,16,2048]{2,1,0:T(8,128)(2,1)}, u32[]{:S(2)}, u32[]{:S(2)}) async-start(bf16[8,16,2048]{2,1,0:T(8,128)(2,1)} %copy.124), calls=%async_computation.11 | async-start | bytes 1048576 | tf_op jit(solution)/shard_map/all_to_all | solution.py:51
  698.7 129.5 %all-reduce.2.cloned.1.call-start = ((), (), s32[]{:S(2)}) async-start(), calls=%async_computation.14 | async-start | bytes 196608 | tf_op jit(solution)/shard_map/psum | solution.py:256
  703.5 126.2 %reduce-scatter.2.cloned.1.call-start = ((), (), s32[]{:S(2)}) async-start(), calls=%async_computation.13 | async-start | bytes 655360 | tf_op jit(solution)/shard_map/reduce_scatter | solution.py:235
  704.4 11.0 %collective-permute-start.3 = (f32[2,2048]{1,0:T(2,128)S(1)}, f32[2,2048]{1,0:T(2,128)S(1)}, u32[]{:S(2)}, u32[]{:S(2)}) collective-permute-start(f32[2,2048]{1,0:T(2,128)S(1)} %slice.390), channel_id=1, source_target_pairs={{1,0},{2,1},{3,2},{4,3},{5,4},{6,5},{7,6},{9,8},{10,9},{11,10},{12... | collective-permute-start | bytes 49160 | tf_op jit(solution)/shard_map/ppermute | solution.py:10
  712.8 6.0 collective-permute-start.4
  714.1 6.3 collective-permute-start.5
  (65 other events, 405.4 us)
Sparse Core Ops, SparseCore 0:
  706.6 121.4 all-reduce.1
Sparse Core Ops, SparseCore 1:
  712.0 20.3 reduce-scatter.1
where the time goes:
time: 846 us; the launch traced here: 839 us
  waiting for transfers between devices  538 us (64%)
  other arithmetic  65.8 us (8%)
  starting transfers between devices  64.8 us (8%)
  matrix products  55.6 us (7%)
  local copies, waits for them, and re-layouts  52.2 us (6%)
  blocking collectives  46 us (5%)
  between operations  17 us (2%)
    all_to_all x3, waiting for transfers between devices, forward_spectrum(): lax.all_to_all(jnp.stack(twiddled), 'ctx', split_axis=1, concat_axis=2, t...  247 us
    all_to_all x3, waiting for transfers between devices, inverse_spectrum(): lax.all_to_all(stacked.astype(jnp.bfloat16), 'ctx', split_axis=1, concat_...  134 us
    psum x1, waiting for transfers between devices, local(): lax.psum((jnp.stack([short_q, short_k, short_v]), skip_grad), ('dp', 'ctx'))  106 us
    psum x1, blocking collectives, local(): lax.psum((jnp.stack([short_q, short_k, short_v]), skip_grad), ('dp', 'ctx'))  46 us
    all_to_all x3, waiting for transfers between devices, to_rows(): return lax.all_to_all(data, 'ctx', split_axis=0, concat_axis=0, tiled=True)  25.7 us
    all_to_all x3, waiting for transfers between devices, to_columns(): return lax.all_to_all(data, 'ctx', split_axis=0, concat_axis=0, tiled=True)  23.9 us
    unnamed x144, local copies, waits for them, and re-layouts  22.3 us
    dot_general x9, matrix products, split_product(): jnp.einsum(form, upper, data_lower, preferred_element_type=jnp.float32)  20 us
  transfers between devices with their start and end apart: 20, of which 13 were waited for; matrix products, arithmetic and copies ran while one was open for 10% of the time, Pallas kernels for 0%

commit v1 on v0

v1 whole, which is shorter than its diff:
```python
import math

import jax
import jax.numpy as jnp
import ml_dtypes
import numpy as np
from jax import lax
from jax.sharding import PartitionSpec as P


def shifted(x, axis, by):
    length = lax.axis_size(axis)
    pairs = [(i, i + by) for i in range(length) if 0 <= i + by < length]
    return lax.ppermute(x, axis, pairs)


def table_halves(table):
    upper = table.astype(ml_dtypes.bfloat16)
    lower = (table - upper.astype(np.float64)).astype(ml_dtypes.bfloat16)
    return jnp.asarray(upper), jnp.asarray(lower)


def split_product(form, table, data):
    upper, lower = table_halves(table)
    wide = jnp.float32
    if data.dtype == jnp.bfloat16:
        total = jnp.einsum(form, upper, data, preferred_element_type=wide)
        return total + jnp.einsum(form, lower, data, preferred_element_type=wide)
    data_upper = lax.optimization_barrier(data.astype(jnp.bfloat16))
    data_lower = (data - data_upper.astype(wide)).astype(jnp.bfloat16)
    total = jnp.einsum(form, upper, data_upper, preferred_element_type=wide)
    total = total + jnp.einsum(form, lower, data_upper, preferred_element_type=wide)
    return total + jnp.einsum(form, upper, data_lower, preferred_element_type=wide)


def factors(size):
    bits = size.bit_length() - 1
    inner = 1 << (bits // 2)
    return size // inner, inner


def twiddles(outer, inner, size):
    phase = 2.0 * np.pi * np.outer(np.arange(outer), np.arange(inner)) / size
    cosine = jnp.asarray(np.cos(phase), jnp.float32)[None, :, :, None]
    sine = jnp.asarray(np.sin(phase), jnp.float32)[None, :, :, None]
    return cosine, sine


def inner_table(inner, sign):
    phase = 2.0 * np.pi * np.outer(np.arange(inner), np.arange(inner)) / inner
    cosine, sine = np.cos(phase), sign * np.sin(phase)
    return np.block([[cosine, sine], [-sine, cosine]])


def fft_forward(signal):
    count, length, lanes = signal.shape
    size = 2 * length
    outer, inner = factors(size)
    half = outer // 2
    phase = 2.0 * np.pi * np.outer(np.arange(outer), np.arange(half)) / outer
    first = np.concatenate([np.cos(phase), -np.sin(phase)], 0)
    stage = split_product("kn,snqb->skqb", first, signal.reshape(count, half, inner, lanes))
    real_part, imag_part = stage[:, :outer], stage[:, outer:]
    cosine, sine = twiddles(outer, inner, size)
    turned = jnp.concatenate(
        [real_part * cosine + imag_part * sine, imag_part * cosine - real_part * sine], 2
    )
    return split_product("ab,skbc->skac", inner_table(inner, 1.0), turned)


def fft_inverse(spectrum, length):
    count, outer, twice, lanes = spectrum.shape
    inner = twice // 2
    size = outer * inner
    half = outer // 2
    stage = split_product("ab,skbc->skac", inner_table(inner, -1.0), spectrum)
    real_part, imag_part = stage[:, :, :inner], stage[:, :, inner:]
    cosine, sine = twiddles(outer, inner, size)
    turned = jnp.concatenate(
        [real_part * cosine - imag_part * sine, imag_part * cosine + real_part * sine], 1
    )
    phase = 2.0 * np.pi * np.outer(np.arange(half), np.arange(outer)) / outer
    last = np.concatenate([np.cos(phase), -np.sin(phase)], 1) / size
    return split_product("nk,skqb->snqb", last, turned).reshape(count, length, lanes)


def spectral_products(spectra):
    inner = spectra.shape[2] // 2
    parts = [(s[:, :inner], s[:, inner:]) for s in (spectra[0], spectra[1], spectra[2])]
    (f_re, f_im), (m_re, m_im), (g_re, g_im) = parts
    conv = jnp.concatenate([m_re * f_re - m_im * f_im, m_re * f_im + m_im * f_re], 1)
    back = jnp.concatenate([g_re * f_re + g_im * f_im, g_im * f_re - g_re * f_im], 1)
    cross = jnp.concatenate([g_re * m_re + g_im * m_im, g_im * m_re - g_re * m_im], 1)
    return jnp.stack([conv, back, cross])


def local(query, keys, values, cotangent, long_filter, short_weights, skip, lengths):
    parts = lax.axis_size("ctx")
    index = lax.axis_index("ctx")
    groups = lax.axis_size("dp")
    q_rows, k_rows, v_rows, c_rows = query[0], keys[0], values[0], cotangent[0]
    rows, chans = q_rows.shape
    taps = short_weights.shape[1]
    head = taps - 1
    seq_len = rows * parts
    lanes = chans // parts
    ext = rows + head
    doc_len = lengths[0]
    starts = jnp.cumsum(doc_len) - doc_len

    position = index * rows + jnp.arange(ext, dtype=jnp.int32)
    begin = jnp.max(jnp.where(starts[None, :] <= position[:, None], starts[None, :], 0), axis=1)
    valid = position[None, :] - jnp.arange(taps, dtype=jnp.int32)[:, None] >= begin[None, :]
    valid_after = valid & (position < seq_len)[None, :]

    prev = shifted((q_rows[rows - head :], k_rows[rows - head :], v_rows[rows - head :]), "ctx", 1)
    nxt = shifted((q_rows[:head], k_rows[:head], v_rows[:head], c_rows[:head]), "ctx", -1)
    padded = [
        jnp.concatenate([prev[i], src, nxt[i]], 0).astype(jnp.float32)
        for i, src in enumerate((q_rows, k_rows, v_rows))
    ]

    def short_forward(wide, weights):
        summed = weights[0] * wide[head : head + ext]
        for offset in range(1, taps):
            begin_at = head - offset
            summed = summed + jnp.where(
                valid[offset][:, None], weights[offset] * wide[begin_at : begin_at + ext], 0.0
            )
        return summed.astype(jnp.bfloat16).astype(jnp.float32)

    q_short = short_forward(padded[0], short_weights[0])
    k_short = short_forward(padded[1], short_weights[1])
    v_short = short_forward(padded[2], short_weights[2])
    upstream = jnp.concatenate([c_rows, nxt[3]], 0).astype(jnp.float32)
    mixed = (k_short * v_short).astype(jnp.bfloat16)
    grad_conv = (upstream * q_short).astype(jnp.bfloat16)
    mixed_wide = mixed.astype(jnp.float32)
    grad_wide = grad_conv.astype(jnp.float32)

    sent = jnp.stack([long_filter, mixed[:rows], grad_conv[:rows]])
    columns = lax.all_to_all(sent, "ctx", 2, 1, tiled=True)
    spectra = fft_forward(columns)
    raw = fft_inverse(spectral_products(spectra), seq_len).astype(jnp.bfloat16)
    raw = jnp.concatenate([raw, jnp.zeros((3, head, lanes), raw.dtype)], 1)
    blocks = jnp.stack([raw[:, j * rows : j * rows + ext] for j in range(parts)], 1)
    back = lax.all_to_all(blocks, "ctx", 1, 3, tiled=True).reshape(3, ext, chans)
    back = back.astype(jnp.float32)

    conv = back[0] + skip * mixed_wide
    gated = (q_short[:rows] * conv[:rows]).astype(jnp.bfloat16)
    grad_qs = upstream * conv
    grad_mixed = back[1] + skip * grad_wide
    grad_ks = grad_mixed * v_short
    grad_vs = grad_mixed * k_short

    def short_backward(wide, grad_short, weights):
        grad_source = weights[0] * grad_short[:rows]
        weight_grads = [jnp.sum(wide[head : head + rows] * grad_short[:rows], axis=0)]
        for offset in range(1, taps):
            later = jnp.where(
                valid_after[offset, offset : offset + rows][:, None],
                grad_short[offset : offset + rows],
                0.0,
            )
            grad_source = grad_source + weights[offset] * later
            masked = jnp.where(valid[offset, :rows][:, None], grad_short[:rows], 0.0)
            begin_at = head - offset
            weight_grads.append(jnp.sum(masked * wide[begin_at : begin_at + rows], axis=0))
        return grad_source, jnp.stack(weight_grads)

    grad_q, short_q = short_backward(padded[0], grad_qs, short_weights[0])
    grad_k, short_k = short_backward(padded[1], grad_ks, short_weights[1])
    grad_v, short_v = short_backward(padded[2], grad_vs, short_weights[2])
    skip_grad = jnp.sum(grad_wide[:rows] * mixed_wide[:rows], axis=0)
    stats = jnp.concatenate(
        [jnp.stack([short_q, short_k, short_v]).reshape(3 * taps, chans), skip_grad[None]], 0
    )
    summed = lax.psum(stats, ("dp", "ctx"))
    filter_part = lax.psum_scatter(back[2, :rows], "dp", scatter_dimension=1, tiled=True)
    scale = 1.0 / (groups * seq_len)
    return (
        gated[None],
        grad_q.astype(jnp.bfloat16)[None],
        grad_k.astype(jnp.bfloat16)[None],
        grad_v.astype(jnp.bfloat16)[None],
        filter_part * scale,
        summed[: 3 * taps].reshape(3, taps, chans) * scale,
        summed[3 * taps] * scale,
    )


def solution(mesh):
    in_specs = (
        P("dp", "ctx", None),
        P("dp", "ctx", None),
        P("dp", "ctx", None),
        P("dp", "ctx", None),
        P("ctx", None),
        P(),
        P(),
        P("dp", None),
    )
    out_specs = (
        P("dp", "ctx", None),
        P("dp", "ctx", None),
        P("dp", "ctx", None),
        P("dp", "ctx", None),
        P("ctx", "dp"),
        P(),
        P(),
    )
    return jax.shard_map(local, mesh=mesh, in_specs=in_specs, out_specs=out_specs, check_vma=False)
```

time: 846 us -> 480 us (0.57)
  waiting for transfers between devices: 538 us -> 156 us
  other arithmetic: 65.8 us -> 115 us
  starting transfers between devices: 64.8 us -> 23.3 us
  local copies, waits for them, and re-layouts: 52.2 us -> 40.1 us
  matrix products: 55.6 us -> 65.5 us
  blocking collectives: 46 us -> 54.8 us
    all_to_all x12 -> x1, waiting for transfers between devices: 430 us -> 36.6 us  [local(): lax.all_to_all(blocks, 'ctx', 1, 3, tiled=True).reshape(3, ext, chans)]
    all_to_all x0 -> x1, blocking collectives: none -> 54.8 us  [local(): columns = lax.all_to_all(sent, 'ctx', 2, 1, tiled=True)]
    psum x1 -> x0, blocking collectives: 46 us -> none  [local(): lax.psum((jnp.stack([short_q, short_k, short_v]), skip_grad), ('dp', 'ctx'))]
    all_to_all x12 -> x1, starting transfers between devices: 49.1 us -> 3.72 us  [local(): lax.all_to_all(blocks, 'ctx', 1, 3, tiled=True).reshape(3, ext, chans)]
    add x7 -> x4, other arithmetic: 14.3 us -> 37.7 us  [the longest x1 26.8 us: split_product(): total + jnp.einsum(form, upper, data_lower, preferred_element_type=wide)]
    convert_element_type x6 -> x3, other arithmetic: 2.07 us -> 21.6 us  [split_product(): data_upper = lax.optimization_barrier(data.astype(jnp.bfloat16))]
    all_to_all x9 -> x2, local copies, waits for them, and re-layouts: 16 us -> 0.93 us  [local(): columns = lax.all_to_all(sent, 'ctx', 2, 1, tiled=True)]
    convert_element_type x9 -> x7, other arithmetic: 1.65 us -> 15 us  [the longest x1 8.81 us: split_product(): data_lower = (data - data_upper.astype(wide)).astype(jnp.bfloat16)]
  transfers between devices with their start and end apart: 20 -> 10, of which waited for: 13 -> 3; matrix products, arithmetic and copies ran while one was open for 10% -> 4% of each run, Pallas kernels for 0% -> 0%
where the time goes in v1:
time: 480 us; the launch traced here: 472 us
  waiting for transfers between devices  156 us (32%)
  other arithmetic  115 us (24%)
  matrix products  65.5 us (14%)
  blocking collectives  54.8 us (11%)
  local copies, waits for them, and re-layouts  40.1 us (8%)
  starting transfers between devices  23.3 us (5%)
  between operations  16.8 us (4%)
    psum x1, waiting for transfers between devices, local(): summed = lax.psum(stats, ('dp', 'ctx'))  118 us
    all_to_all x1, blocking collectives, local(): columns = lax.all_to_all(sent, 'ctx', 2, 1, tiled=True)  54.8 us
    all_to_all x1, waiting for transfers between devices, local(): lax.all_to_all(blocks, 'ctx', 1, 3, tiled=True).reshape(3, ext, chans)  36.6 us
    add x1, other arithmetic, split_product(): total + jnp.einsum(form, upper, data_lower, preferred_element_type=wide)  26.8 us
    dot_general x3, matrix products, split_product(): jnp.einsum(form, upper, data_lower, preferred_element_type=wide)  22.9 us
    dot_general x3, matrix products, split_product(): jnp.einsum(form, lower, data_upper, preferred_element_type=wide)  21.8 us
    convert_element_type x3, other arithmetic, split_product(): data_upper = lax.optimization_barrier(data.astype(jnp.bfloat16))  21.6 us
    ppermute x7, starting transfers between devices, shifted(): return lax.ppermute(x, axis, pairs)  19.5 us
  transfers between devices with their start and end apart: 10, of which 3 were waited for; matrix products, arithmetic and copies ran while one was open for 4% of the time, Pallas kernels for 0%

profile of v1, /device:TPU:0, one launch (start us, length us, event | category | flops | bytes accessed | tf_op | source)
XLA Modules:
  0.0 471.9 jit_solution(2773663166921018954)
XLA Ops:
  8.9 4.9 %collective-permute-start.4 = (bf16[2,2048]{1,0:T(2,128)(2,1)S(1)}, bf16[2,2048]{1,0:T(2,128)(2,1)S(1)}, u32[]{:S(2)}, u32[]{:S(2)}) collective-permute-start(bf16[2,2048]{1,0:T(2,128)(2,1)S(1)} %get-tuple-element.58), channel_id=1, source_target_pairs={{0,1},{1,2},{2,3},{3,4},{4,5},{5,6},{6,7},{8,9},{9,10},{10,11},{11... | collective-permute-start | bytes 24584 | tf_op jit(solution)/shard_map/ppermute | solution.py:14
  15.8 4.5 collective-permute-start.2
  22.5 5.0 %collective-permute-start = (bf16[2,2048]{1,0:T(2,128)(2,1)S(1)}, bf16[2,2048]{1,0:T(2,128)(2,1)S(1)}, u32[]{:S(2)}, u32[]{:S(2)}) collective-permute-start(bf16[2,2048]{1,0:T(2,128)(2,1)S(1)} %get-tuple-element.62), channel_id=1, source_target_pairs={{0,1},{1,2},{2,3},{3,4},{4,5},{5,6},{6,7},{8,9},{9,10},{10,11},{11... | collective-permute-start | bytes 24584 | tf_op jit(solution)/shard_map/ppermute | solution.py:14
  47.6 54.8 %all_to_all.24 = bf16[3,128,2048]{1,0,2:T(4,128)(2,1)S(1)} all-to-all(bf16[3,128,2048]{1,0,2:T(4,128)(2,1)S(1)} %copy.95), channel_id=1, replica_groups=mesh['dp'=4,'ctx'=8] {'ctx'}, dimensions={2} | all-to-all | bytes 3145728 | tf_op jit(solution)/shard_map/all_to_all | solution.py:142
  107.5 5.4 %multiply_add_fusion.1 = (f32[3,64,32,256]{3,1,2,0:T(8,128)}, f32[3,64,32,256]{3,1,2,0:T(8,128)}) fusion(f32[3,128,32,256]{3,1,2,0:T(8,128)S(1)} %add_bitcast_fusion.1, f32[64,32]{0,1:T(8,128)S(1)} %copy-done.44, f32[64,32]{0,1:T(8,128)S(1)} %copy-done.45), kind=kLoop, calls=%fused_computation.20 | loop fusion | flops 9437184 | bytes 25182208 | tf_op jit(solution)/shard_map/add | solution.py:66
  112.9 7.9 %fusion.2 = bf16[3,64,64,256]{3,1,2,0:T(8,128)(2,1)} fusion(f32[3,64,32,256]{3,1,2,0:T(8,128)} %get-tuple-element.39, f32[3,64,32,256]{3,1,2,0:T(8,128)} %get-tuple-element.38), kind=kLoop, calls=%fused_computation.12 | loop fusion | flops 3145728 | bytes 18874368 | tf_op jit(solution)/shard_map/convert_element_type | solution.py:29
  120.8 8.8 %subtract_convert_fusion.2 = bf16[3,64,64,256]{3,1,2,0:T(8,128)(2,1)S(1)} fusion(bf16[3,64,64,256]{3,1,2,0:T(8,128)(2,1)} %fusion.2, f32[3,64,32,256]{3,1,2,0:T(8,128)} %get-tuple-element.39, f32[3,64,32,256]{3,1,2,0:T(8,128)} %get-tuple-element.38), kind=kLoop, calls=%fused_computation.9 | loop fusion | flops 12582912 | bytes 25165824 | tf_op jit(solution)/shard_map/convert_element_type | solution.py:30
  129.6 9.5 %fusion.8 = f32[3,64,256,64]{2,3,1,0:T(8,128)} fusion(bf16[64,64,1,1]{1,0,3,2:T(8,128)(2,1)S(1)} %copy-done.46, bf16[3,64,64,256]{3,1,2,0:T(8,128)(2,1)S(1)} %copy-done.1), kind=kOutput, calls=%fused_computation.22 | convolution fusion | flops 402653184 | bytes 18882560 | tf_op jit(solution)/shard_map/ab,skbc->skac/dot_general | solution.py:31
  139.1 9.5 %fusion.5 = f32[3,64,256,64]{2,3,1,0:T(8,128)} fusion(bf16[64,64,1,1]{1,0,3,2:T(8,128)(2,1)S(1)} %copy-done.46, bf16[3,64,64,256]{3,1,2,0:T(8,128)(2,1)S(1)} %subtract_convert_fusion.2), kind=kOutput, calls=%fused_computation.15 | convolution fusion | flops 402653184 | bytes 18882560 | tf_op jit(solution)/shard_map/ab,skbc->skac/dot_general | solution.py:33
  148.6 14.4 %add_bitcast_fusion = f32[3,64,64,256]{3,2,1,0:T(8,128)} fusion(f32[3,64,256,64]{2,3,1,0:T(8,128)} %fusion.5, f32[3,64,256,64]{2,3,1,0:T(8,128)} %fusion.8, bf16[64,64,1,1]{1,0,3,2:T(8,128)(2,1)S(1)} %copy-done.50, bf16[3,64,64,256]{3,1,2,0:T(8,128)(2,1)S(1)} %copy-done.1), kind=kOutput, calls=%fused_computation.8 | convolution fusion | flops 408944640 | bytes 44048384 | tf_op jit(solution)/shard_map/ab,skbc->skac/dot_general | solution.py:32
  163.0 9.9 %slice_bitcast_fusion.1 = (f32[64,64,256]{2,1,0:T(8,128)S(1)}, f32[64,64,256]{2,1,0:T(8,128)}, f32[64,64,256]{2,1,0:T(8,128)}) fusion(f32[3,64,64,256]{3,2,1,0:T(8,128)} %add_bitcast_fusion), kind=kLoop, calls=%fused_computation.27 | loop fusion | bytes 25165824 | tf_op jit(solution)/shard_map/squeeze | solution.py:89
  173.0 5.5 %multiply_add_fusion.3 = (f32[64,32,256]{2,1,0:T(8,128)}, f32[64,32,256]{2,1,0:T(8,128)}) fusion(f32[64,64,256]{2,1,0:T(8,128)} %get-tuple-element.41, f32[64,64,256]{2,1,0:T(8,128)S(1)} %get-tuple-element.40), kind=kLoop, calls=%fused_computation.37 | loop fusion | flops 3145728 | bytes 12582912 | tf_op jit(solution)/shard_map/add | solution.py:92
  178.4 5.8 %multiply_subtract_fusion.4 = (f32[64,32,256]{2,1,0:T(8,128)}, f32[64,32,256]{2,1,0:T(8,128)}, f32[64,32,256]{2,1,0:T(8,128)S(1)}, f32[64,32,256]{2,1,0:T(8,128)S(1)}) fusion(f32[64,64,256]{2,1,0:T(8,128)S(1)} %get-tuple-element.40, f32[64,64,256]{2,1,0:T(8,128)} %get-tuple-element.42, f32[64,64,256]{2,1,0:T(8,128)S(1)} %copy-done.8), kind=kLoop, calls=%fused_computation.39 | loop fusion | flops 6291456 | bytes 20971520 | tf_op jit(solution)/shard_map/sub | solution.py:91
  184.2 4.8 %maximum_bitcast_fusion.1 = f32[1,64,64,256]{3,2,1,0:T(8,128)} fusion(f32[64,32,256]{2,1,0:T(8,128)} %get-tuple-element.46, f32[64,32,256]{2,1,0:T(8,128)} %get-tuple-element.45), kind=kLoop, calls=%fused_computation.30 | loop fusion | flops 1048576 | bytes 8388608 | tf_op jit(solution)/shard_map/stack | solution.py:94
  193.8 5.4 %fusion.3 = bf16[3,64,64,256]{3,2,1,0:T(8,128)(2,1)S(1)} fusion(f32[1,64,64,256]{3,2,1,0:T(8,128)} %maximum_bitcast_fusion.2, f32[1,64,64,256]{3,2,1,0:T(8,128)} %maximum_bitcast_fusion.1, f32[1,64,64,256]{3,2,1,0:T(8,128)} %maximum_bitcast_fusion), kind=kLoop, calls=%fused_computation.13 | loop fusion | flops 6291456 | bytes 18874368 | tf_op jit(solution)/shard_map/convert_element_type | solution.py:29
  199.2 5.9 %fusion.4 = f32[3,64,256,64]{2,3,1,0:T(8,128)S(1)} fusion(bf16[64,64,1,1]{1,0,3,2:T(8,128)(2,1)S(1)} %copy-done.43, bf16[3,64,64,256]{3,2,1,0:T(8,128)(2,1)S(1)} %fusion.3, f32[1,64,64,256]{3,2,1,0:T(8,128)} %maximum_bitcast_fusion.2, f32[1,64,64,256]{3,2,1,0:T(8,128)} %maximum_bitcast_fusion.1, f32[1,64,64,256]{3,2,1,0:T(8,128)} %maximum_bitcast_fusion), kind=kOutput, calls=%fused_computation.14 | convolution fusion | flops 418381824 | bytes 31465472 | tf_op jit(solution)/shard_map/ab,skbc->skac/dot_general | solution.py:33
  205.1 6.4 %fusion.86 = f32[3,64,256,64]{2,3,1,0:T(8,128)} fusion(bf16[64,64,1,1]{1,0,3,2:T(8,128)(2,1)S(1)} %copy-done.43, bf16[3,64,64,256]{3,2,1,0:T(8,128)(2,1)S(1)} %fusion.3), kind=kOutput, calls=%fused_computation.185 | convolution fusion | flops 402653184 | bytes 18882560 | tf_op jit(solution)/shard_map/ab,skbc->skac/dot_general | solution.py:31
  211.5 6.3 %fusion.87 = f32[3,64,256,64]{2,3,1,0:T(8,128)} fusion(bf16[64,64,1,1]{1,0,3,2:T(8,128)(2,1)S(1)} %copy-done.53, bf16[3,64,64,256]{3,2,1,0:T(8,128)(2,1)S(1)} %fusion.3), kind=kOutput, calls=%fused_computation.186 | convolution fusion | flops 402653184 | bytes 18882560 | tf_op jit(solution)/shard_map/ab,skbc->skac/dot_general | solution.py:32
  217.8 26.8 %fusion = f32[3,64,64,256]{3,1,2,0:T(8,128)} fusion(f32[3,64,256,64]{2,3,1,0:T(8,128)S(1)} %fusion.4, f32[3,64,256,64]{2,3,1,0:T(8,128)} %fusion.87, f32[3,64,256,64]{2,3,1,0:T(8,128)} %fusion.86), kind=kLoop, calls=%fused_computation.4 | loop fusion | flops 6291456 | bytes 50331648 | tf_op jit(solution)/shard_map/add | solution.py:33
  244.6 8.3 %multiply_subtract_fusion = (f32[3,64,32,256]{3,1,2,0:T(8,128)}, f32[3,64,32,256]{3,1,2,0:T(8,128)}) fusion(f32[3,64,64,256]{3,1,2,0:T(8,128)} %fusion, f32[64,32]{0,1:T(8,128)S(1)} %copy-done.44, f32[64,32]{0,1:T(8,128)S(1)} %copy-done.45), kind=kLoop, calls=%fused_computation.18 | loop fusion | flops 9437184 | bytes 25182208 | tf_op jit(solution)/shard_map/sub | solution.py:80
  252.9 8.3 %fusion.1 = bf16[3,128,32,256]{3,1,2,0:T(8,128)(2,1)} fusion(f32[3,64,32,256]{3,1,2,0:T(8,128)} %get-tuple-element.37, f32[3,64,32,256]{3,1,2,0:T(8,128)} %get-tuple-element.36), kind=kLoop, calls=%fused_computation.11 | loop fusion | flops 12582912 | bytes 18874368 | tf_op jit(solution)/shard_map/convert_element_type | solution.py:29
  261.2 7.6 %fusion.7 = f32[3,32,256,32]{2,3,1,0:T(8,128)S(1)} fusion(bf16[32,128,1,1]{1,0,3,2:T(8,128)(2,1)S(1)} %copy-done.49, bf16[3,128,32,256]{3,1,2,0:T(8,128)(2,1)} %fusion.1, f32[3,64,32,256]{3,1,2,0:T(8,128)} %get-tuple-element.37, f32[3,64,32,256]{3,1,2,0:T(8,128)} %get-tuple-element.36), kind=kOutput, calls=%fused_computation.21 | convolution fusion | flops 213909504 | bytes 22028288 | tf_op jit(solution)/shard_map/nk,skqb->snqb/dot_general | solution.py:33
  283.2 36.6 %all-to-all-done.1 = bf16[3,8,130,256]{3,2,0,1:T(8,128)(2,1)S(1)} async-done(((bf16[3,8,130,256]{3,2,0,1:T(8,128)(2,1)}), bf16[3,8,130,256]{3,2,0,1:T(8,128)(2,1)S(1)}, u32[]{:S(2)}, u32[]{:S(2)}) %all-to-all-start.1) | async-done | bytes 1597472 | tf_op jit(solution)/shard_map/all_to_all | solution.py:147
  341.2 118.1 %all-reduce.3.cloned.1.call-done = f32[10,2048]{1,0:T(8,128)} async-done(((f32[10,2048]{1,0:T(8,128)}), f32[10,2048]{1,0:T(8,128)}) %all-reduce.3.cloned.1.call-update) | async-done | bytes 81936 | tf_op jit(solution)/shard_map/psum | solution.py:179
  (200 shorter events, 74.7 us)
Async XLA Ops:
  8.0 27.4 %copy-start.22 = (bf16[1,128,2048]{2,1,0:T(8,128)(2,1)S(1)}, bf16[1,128,2048]{2,1,0:T(8,128)(2,1)}, u32[]{:S(2)}) copy-start(bf16[1,128,2048]{2,1,0:T(8,128)(2,1)} %param.22) | copy-start | bytes 1572868
  8.9 26.6 %collective-permute-start.4 = (bf16[2,2048]{1,0:T(2,128)(2,1)S(1)}, bf16[2,2048]{1,0:T(2,128)(2,1)S(1)}, u32[]{:S(2)}, u32[]{:S(2)}) collective-permute-start(bf16[2,2048]{1,0:T(2,128)(2,1)S(1)} %get-tuple-element.58), channel_id=1, source_target_pairs={{0,1},{1,2},{2,3},{3,4},{4,5},{5,6},{6,7},{8,9},{9,10},{10,11},{11... | collective-permute-start | bytes 24584 | tf_op jit(solution)/shard_map/ppermute | solution.py:14
  13.7 21.7 %collective-permute-start.5 = (bf16[2,2048]{1,0:T(2,128)(2,1)S(1)}, bf16[2,2048]{1,0:T(2,128)(2,1)S(1)}, u32[]{:S(2)}, u32[]{:S(2)}) collective-permute-start(bf16[2,2048]{1,0:T(2,128)(2,1)S(1)} %get-tuple-element.59), channel_id=1, source_target_pairs={{1,0},{2,1},{3,2},{4,3},{5,4},{6,5},{7,6},{9,8},{10,9},{11,10},{12... | collective-permute-start | bytes 24584 | tf_op jit(solution)/shard_map/ppermute | solution.py:14
  15.8 15.7 %collective-permute-start.2 = (bf16[2,2048]{1,0:T(2,128)(2,1)S(1)}, bf16[2,2048]{1,0:T(2,128)(2,1)S(1)}, u32[]{:S(2)}, u32[]{:S(2)}) collective-permute-start(bf16[2,2048]{1,0:T(2,128)(2,1)S(1)} %get-tuple-element.60), channel_id=1, source_target_pairs={{0,1},{1,2},{2,3},{3,4},{4,5},{5,6},{6,7},{8,9},{9,10},{10,11},{11... | collective-permute-start | bytes 24584 | tf_op jit(solution)/shard_map/ppermute | solution.py:14
  20.4 12.5 %collective-permute-start.3 = (bf16[2,2048]{1,0:T(2,128)(2,1)S(1)}, bf16[2,2048]{1,0:T(2,128)(2,1)S(1)}, u32[]{:S(2)}, u32[]{:S(2)}) collective-permute-start(bf16[2,2048]{1,0:T(2,128)(2,1)S(1)} %get-tuple-element.61), channel_id=1, source_target_pairs={{1,0},{2,1},{3,2},{4,3},{5,4},{6,5},{7,6},{9,8},{10,9},{11,10},{12... | collective-permute-start | bytes 24584 | tf_op jit(solution)/shard_map/ppermute | solution.py:14
  22.5 15.7 %collective-permute-start = (bf16[2,2048]{1,0:T(2,128)(2,1)S(1)}, bf16[2,2048]{1,0:T(2,128)(2,1)S(1)}, u32[]{:S(2)}, u32[]{:S(2)}) collective-permute-start(bf16[2,2048]{1,0:T(2,128)(2,1)S(1)} %get-tuple-element.62), channel_id=1, source_target_pairs={{0,1},{1,2},{2,3},{3,4},{4,5},{5,6},{6,7},{8,9},{9,10},{10,11},{11... | collective-permute-start | bytes 24584 | tf_op jit(solution)/shard_map/ppermute | solution.py:14
  30.8 7.3 %copy-start.25 = (f32[1,1,2048]{2,1,0:T(1,128)}, f32[1,1,2048]{2,1,0:T(1,128)S(1)}, u32[]{:S(2)}) copy-start(f32[1,1,2048]{2,1,0:T(1,128)S(1)} %get-tuple-element.65) | copy-start | bytes 24580
  30.8 7.3 %copy-start.27 = (f32[1,1,2048]{2,1,0:T(1,128)}, f32[1,1,2048]{2,1,0:T(1,128)S(1)}, u32[]{:S(2)}) copy-start(f32[1,1,2048]{2,1,0:T(1,128)S(1)} %get-tuple-element.66) | copy-start | bytes 24580
  30.8 7.3 %copy-start.29 = (f32[1,1,2048]{2,1,0:T(1,128)}, f32[1,1,2048]{2,1,0:T(1,128)S(1)}, u32[]{:S(2)}) copy-start(f32[1,1,2048]{2,1,0:T(1,128)S(1)} %get-tuple-element.67) | copy-start | bytes 24580
  30.8 7.3 %copy-start.31 = (f32[1,1,2048]{2,1,0:T(1,128)}, f32[1,1,2048]{2,1,0:T(1,128)S(1)}, u32[]{:S(2)}) copy-start(f32[1,1,2048]{2,1,0:T(1,128)S(1)} %get-tuple-element.64) | copy-start | bytes 24580
  30.8 7.3 %copy-start.33 = (f32[1,1,2048]{2,1,0:T(1,128)}, f32[1,1,2048]{2,1,0:T(1,128)S(1)}, u32[]{:S(2)}) copy-start(f32[1,1,2048]{2,1,0:T(1,128)S(1)} %get-tuple-element.71) | copy-start | bytes 24580
  30.9 9.1 %copy-start.37 = (f32[1,1,2048]{2,1,0:T(1,128)}, f32[1,1,2048]{2,1,0:T(1,128)S(1)}, u32[]{:S(2)}) copy-start(f32[1,1,2048]{2,1,0:T(1,128)S(1)} %get-tuple-element.68) | copy-start | bytes 24580
  30.9 9.1 %copy-start.39 = (f32[1,1,2048]{2,1,0:T(1,128)}, f32[1,1,2048]{2,1,0:T(1,128)S(1)}, u32[]{:S(2)}) copy-start(f32[1,1,2048]{2,1,0:T(1,128)S(1)} %get-tuple-element.69) | copy-start | bytes 24580
  30.9 9.1 %copy-start.41 = (f32[1,1,2048]{2,1,0:T(1,128)}, f32[1,1,2048]{2,1,0:T(1,128)S(1)}, u32[]{:S(2)}) copy-start(f32[1,1,2048]{2,1,0:T(1,128)S(1)} %get-tuple-element.70) | copy-start | bytes 24580
  31.6 6.6 %collective-permute-start.1 = (bf16[2,2048]{1,0:T(2,128)(2,1)S(1)}, bf16[2,2048]{1,0:T(2,128)(2,1)S(1)}, u32[]{:S(2)}, u32[]{:S(2)}) collective-permute-start(bf16[2,2048]{1,0:T(2,128)(2,1)S(1)} %get-tuple-element.63), channel_id=1, source_target_pairs={{1,0},{2,1},{3,2},{4,3},{5,4},{6,5},{7,6},{9,8},{10,9},{11,10},{12... | collective-permute-start | bytes 24584 | tf_op jit(solution)/shard_map/ppermute | solution.py:14
  32.9 7.1 %collective-permute-start.6 = (bf16[2,2048]{1,0:T(2,128)(2,1)S(1)}, bf16[2,2048]{1,0:T(2,128)(2,1)S(1)}, u32[]{:S(2)}, u32[]{:S(2)}) collective-permute-start(bf16[2,2048]{1,0:T(2,128)(2,1)S(1)} %slice_bitcast_fusion.13), channel_id=1, source_target_pairs={{1,0},{2,1},{3,2},{4,3},{5,4},{6,5},{7,6},{9,8},{10,9},{11,10},{12... | collective-permute-start | bytes 24584 | tf_op jit(solution)/shard_map/ppermute | solution.py:14
  120.8 8.8 %copy-start.1 = (bf16[3,64,64,256]{3,1,2,0:T(8,128)(2,1)S(1)}, bf16[3,64,64,256]{3,1,2,0:T(8,128)(2,1)}, u32[]{:S(2)}) copy-start(bf16[3,64,64,256]{3,1,2,0:T(8,128)(2,1)} %fusion.2) | copy-start | bytes 18874372
  120.8 8.8 %copy-start.46 = (bf16[64,64,1,1]{1,0,3,2:T(8,128)(2,1)S(1)}, bf16[64,64,1,1]{1,0,3,2:T(8,128)(2,1)}, u32[]{:S(2)}) copy-start(bf16[64,64,1,1]{1,0,3,2:T(8,128)(2,1)} %constant.62) | copy-start | bytes 24580
  139.1 9.5 %copy-start.50 = (bf16[64,64,1,1]{1,0,3,2:T(8,128)(2,1)S(1)}, bf16[64,64,1,1]{1,0,3,2:T(8,128)(2,1)}, u32[]{:S(2)}) copy-start(bf16[64,64,1,1]{1,0,3,2:T(8,128)(2,1)} %constant.63) | copy-start | bytes 24580
  252.9 8.3 %copy-start.49 = (bf16[32,128,1,1]{1,0,3,2:T(8,128)(2,1)S(1)}, bf16[32,128,1,1]{1,0,3,2:T(8,128)(2,1)}, u32[]{:S(2)}) copy-start(bf16[32,128,1,1]{1,0,3,2:T(8,128)(2,1)} %constant.66) | copy-start | bytes 24580
  261.1 8.3 %copy-start = (bf16[3,128,32,256]{3,1,2,0:T(8,128)(2,1)S(1)}, bf16[3,128,32,256]{3,1,2,0:T(8,128)(2,1)}, u32[]{:S(2)}) copy-start(bf16[3,128,32,256]{3,1,2,0:T(8,128)(2,1)} %fusion.1) | copy-start | bytes 18874372
  278.0 41.8 %all-to-all-start.1 = ((bf16[3,8,130,256]{3,2,0,1:T(8,128)(2,1)}), bf16[3,8,130,256]{3,2,0,1:T(8,128)(2,1)S(1)}, u32[]{:S(2)}, u32[]{:S(2)}) async-start(bf16[3,8,130,256]{3,2,0,1:T(8,128)(2,1)} %fusion.67), calls=%async_computation.1 | async-start | bytes 3342336 | tf_op jit(solution)/shard_map/all_to_all | solution.py:147
  281.7 177.6 %all-reduce.3.cloned.1.call-start = ((), (), s32[]{:S(2)}) async-start(), calls=%async_computation.4 | async-start | bytes 262144 | tf_op jit(solution)/shard_map/psum | solution.py:179
  337.9 124.5 %reduce-scatter.2.cloned.1.call-start = ((), (), s32[]{:S(2)}) async-start(), calls=%async_computation.3 | async-start | bytes 1310720 | tf_op jit(solution)/shard_map/reduce_scatter | solution.py:180
  (45 other events, 116.6 us)
Sparse Core Ops, SparseCore 0:
  338.0 121.2 all-reduce.2
Sparse Core Ops, SparseCore 1:
  340.9 23.7 reduce-scatter.1

commit v2 on v1

--- a/solution.py
+++ b/solution.py
@@ -20,9 +20,11 @@
     return jnp.asarray(upper), jnp.asarray(lower)
 
 
-def split_product(form, table, data):
+def split_product(form, table, data, exact=True):
     upper, lower = table_halves(table)
     wide = jnp.float32
+    if not exact:
+        return jnp.einsum(form, upper, data.astype(jnp.bfloat16), preferred_element_type=wide)
     if data.dtype == jnp.bfloat16:
         total = jnp.einsum(form, upper, data, preferred_element_type=wide)
         return total + jnp.einsum(form, lower, data, preferred_element_type=wide)
@@ -65,7 +67,7 @@
     turned = jnp.concatenate(
         [real_part * cosine + imag_part * sine, imag_part * cosine - real_part * sine], 2
     )
-    return split_product("ab,skbc->skac", inner_table(inner, 1.0), turned)
+    return split_product("ab,skbc->skac", inner_table(inner, 1.0), turned, exact=False)
 
 
 def fft_inverse(spectrum, length):
@@ -73,7 +75,7 @@
     inner = twice // 2
     size = outer * inner
     half = outer // 2
-    stage = split_product("ab,skbc->skac", inner_table(inner, -1.0), spectrum)
+    stage = split_product("ab,skbc->skac", inner_table(inner, -1.0), spectrum, exact=False)
     real_part, imag_part = stage[:, :, :inner], stage[:, :, inner:]
     cosine, sine = twiddles(outer, inner, size)
     turned = jnp.concatenate(
@@ -81,7 +83,7 @@
     )
     phase = 2.0 * np.pi * np.outer(np.arange(half), np.arange(outer)) / outer
     last = np.concatenate([np.cos(phase), -np.sin(phase)], 1) / size
-    return split_product("nk,skqb->snqb", last, turned).reshape(count, length, lanes)
+    return split_product("nk,skqb->snqb", last, turned, exact=False).reshape(count, length, lanes)
 
 
 def spectral_products(spectra):
@@ -92,6 +94,31 @@
     back = jnp.concatenate([g_re * f_re + g_im * f_im, g_im * f_re - g_re * f_im], 1)
     cross = jnp.concatenate([g_re * m_re + g_im * m_im, g_im * m_re - g_re * m_im], 1)
     return jnp.stack([conv, back, cross])
+
+
+def butterfly_sum(data, axis):
+    size = lax.axis_size(axis)
+    step = 1
+    while step < size:
+        data = data + lax.ppermute(data, axis, [(i, i ^ step) for i in range(size)])
+        step *= 2
+    return data
+
+
+def halving_scatter(data, axis):
+    size = lax.axis_size(axis)
+    index = lax.axis_index(axis)
+    rows, chans = data.shape
+    blocks = data.reshape(rows, size, chans // size)
+    step = size // 2
+    while step >= 1:
+        half = blocks.shape[1] // 2
+        upper = (index // step) % 2 == 1
+        keep = jnp.where(upper, blocks[:, half:], blocks[:, :half])
+        give = jnp.where(upper, blocks[:, :half], blocks[:, half:])
+        blocks = keep + lax.ppermute(give, axis, [(i, i ^ step) for i in range(size)])
+        step //= 2
+    return blocks.reshape(rows, chans // size)
 
 
 def local(query, keys, values, cotangent, long_filter, short_weights, skip, lengths):
@@ -113,8 +140,8 @@
     valid = position[None, :] - jnp.arange(taps, dtype=jnp.int32)[:, None] >= begin[None, :]
     valid_after = valid & (position < seq_len)[None, :]
 
-    prev = shifted((q_rows[rows - head :], k_rows[rows - head :], v_rows[rows - head :]), "ctx", 1)
-    nxt = shifted((q_rows[:head], k_rows[:head], v_rows[:head], c_rows[:head]), "ctx", -1)
+    prev = shifted(jnp.stack([a[rows - head :] for a in (q_rows, k_rows, v_rows)]), "ctx", 1)
+    nxt = shifted(jnp.stack([a[:head] for a in (q_rows, k_rows, v_rows, c_rows)]), "ctx", -1)
     padded = [
         jnp.concatenate([prev[i], src, nxt[i]], 0).astype(jnp.float32)
         for i, src in enumerate((q_rows, k_rows, v_rows))
@@ -176,8 +203,8 @@
     stats = jnp.concatenate(
         [jnp.stack([short_q, short_k, short_v]).reshape(3 * taps, chans), skip_grad[None]], 0
     )
-    summed = lax.psum(stats, ("dp", "ctx"))
-    filter_part = lax.psum_scatter(back[2, :rows], "dp", scatter_dimension=1, tiled=True)
+    summed = butterfly_sum(butterfly_sum(stats, "ctx"), "dp")
+    filter_part = halving_scatter(back[2, :rows], "dp")
     scale = 1.0 / (groups * seq_len)
     return (
         gated[None],

time: 480 us -> 262 us (0.55)
  waiting for transfers between devices: 156 us -> 61.1 us
  other arithmetic: 115 us -> 41.3 us
  matrix products: 65.5 us -> 23.2 us
  local copies, waits for them, and re-layouts: 40.1 us -> 61.7 us
  between operations: 16.8 us -> 1.77 us
  starting transfers between devices: 23.3 us -> 15 us
    psum x1 -> x0, waiting for transfers between devices: 118 us -> none  [local(): summed = lax.psum(stats, ('dp', 'ctx'))]
    dot_general x9 -> x3, matrix products: 61.6 us -> 16.4 us  [split_product(): jnp.einsum(form, upper, data.astype(jnp.bfloat16), preferred_element_type...]
    add x3 -> x6, other arithmetic: 37.6 us -> 0.16 us  [the longest x5 0.09 us: butterfly_sum(): data = data + lax.ppermute(data, axis, [(i, i ^ step) for i in range(size)])]
    convert_element_type x4 -> x0, other arithmetic: 30.4 us -> none  [the longest x3 21.6 us: split_product(): data_upper = lax.optimization_barrier(data.astype(jnp.bfloat16))]
    ppermute x0 -> x7, waiting for transfers between devices: none -> 22.9 us  [the longest x5 22 us: butterfly_sum(): data = data + lax.ppermute(data, axis, [(i, i ^ step) for i in range(size)])]
    another operation x1 -> x7, other arithmetic: 0.84 us -> 17.8 us
    dot_general x0 -> x1, local copies, waits for them, and re-layouts: none -> 16.3 us  [split_product(): jnp.einsum(form, upper, data.astype(jnp.bfloat16), preferred_element_type...]
    sub x2 -> x0, other arithmetic: 14.1 us -> none  [the longest x1 8.31 us: fft_inverse(): real_part * cosine - imag_part * sine]
  transfers between devices with their start and end apart: 10 -> 10, of which waited for: 3 -> 6; matrix products, arithmetic and copies ran while one was open for 4% -> 6% of each run, Pallas kernels for 0% -> 0%
where the time goes in v2:
time: 262 us; the launch traced here: 257 us
  local copies, waits for them, and re-layouts  61.7 us (24%)
  waiting for transfers between devices  61.1 us (23%)
  blocking collectives  53.1 us (20%)
  other arithmetic  41.3 us (16%)
  matrix products  23.2 us (9%)
  starting transfers between devices  15 us (6%)
    all_to_all x1, blocking collectives, local(): columns = lax.all_to_all(sent, 'ctx', 2, 1, tiled=True)  53.1 us
    all_to_all x1, waiting for transfers between devices, local(): lax.all_to_all(blocks, 'ctx', 1, 3, tiled=True).reshape(3, ext, chans)  36.4 us
    ppermute x5, waiting for transfers between devices, butterfly_sum(): data = data + lax.ppermute(data, axis, [(i, i ^ step) for i in range(size)])  22 us
    another operation x5, other arithmetic  17.7 us
    dot_general x3, matrix products, split_product(): jnp.einsum(form, upper, data.astype(jnp.bfloat16), preferred_element_type...  16.4 us
    dot_general x1, local copies, waits for them, and re-layouts, split_product(): jnp.einsum(form, upper, data.astype(jnp.bfloat16), preferred_element_type...  16.3 us
    unnamed x66, local copies, waits for them, and re-layouts  12.9 us
    squeeze x1, local copies, waits for them, and re-layouts, spectral_products(): spectra[0]  9.65 us
  transfers between devices with their start and end apart: 10, of which 6 were waited for; matrix products, arithmetic and copies ran while one was open for 6% of the time, Pallas kernels for 0%

profile of v2, /device:TPU:0, one launch (start us, length us, event | category | flops | bytes accessed | tf_op | source)
XLA Modules:
  0.0 257.2 jit_solution(18214595631692640615)
XLA Ops:
  3.1 4.9 %collective-permute-start = (bf16[3,2,2048]{2,1,0:T(2,128)(2,1)S(1)}, bf16[3,2,2048]{2,1,0:T(2,128)(2,1)S(1)}, u32[]{:S(2)}, u32[]{:S(2)}) collective-permute-start(bf16[3,2,2048]{2,1,0:T(2,128)(2,1)S(1)} %pad_maximum_fusion.6), channel_id=1, source_target_pairs={{0,1},{1,2},{2,3},{3,4},{4,5},{5,6},{6,7},{8,9},{9,10},{10,11},{11... | collective-permute-start | bytes 73736 | tf_op jit(solution)/shard_map/ppermute | solution.py:14
  16.3 2.4 fusion.86
  19.9 2.0 fusion.83
  24.1 4.2 %copy.97 = bf16[3,128,2048]{1,0,2:T(4,128)(2,1)} copy(bf16[3,128,2048]{2,1,0:T(8,128)(2,1)} %pad_maximum_fusion.1) | data formatting | bytes 3145728 | tf_op jit(solution)/shard_map/stack | solution.py:168
  28.3 53.1 %all_to_all.24 = bf16[3,128,2048]{1,0,2:T(4,128)(2,1)S(1)} all-to-all(bf16[3,128,2048]{1,0,2:T(4,128)(2,1)} %copy.97), channel_id=1, replica_groups=mesh['dp'=4,'ctx'=8] {'ctx'}, dimensions={2} | all-to-all | bytes 3145728 | tf_op jit(solution)/shard_map/all_to_all | solution.py:169
  82.8 2.6 %copy.99 = bf16[3,8,128,256]{3,2,1,0:T(8,128)(2,1)} copy(bf16[3,8,128,256]{2,3,1,0:T(8,128)(2,1)} %bitcast.184) | data formatting | bytes 3145728 | tf_op jit(solution)/shard_map/all_to_all | solution.py:169
  85.4 3.2 %fusion.22 = f32[3,32,256,128]{2,3,1,0:T(8,128)S(1)} fusion(bf16[128,32,1,1]{0,1,3,2:T(8,128)(2,1)S(1)} %copy-done.21, bf16[3,32,32,256]{3,2,1,0:T(8,128)(2,1)} %bitcast.172), kind=kOutput, calls=%fused_computation.43 | convolution fusion | flops 201326592 | bytes 14163968 | tf_op jit(solution)/shard_map/kn,snqb->skqb/dot_general | solution.py:29
  88.7 3.6 %add_bitcast_fusion = f32[3,128,32,256]{3,1,2,0:T(8,128)S(1)} fusion(f32[3,32,256,128]{2,3,1,0:T(8,128)S(1)} %fusion.22, bf16[128,32,1,1]{0,1,3,2:T(8,128)(2,1)S(1)} %copy-done.22, bf16[3,32,32,256]{3,2,1,0:T(8,128)(2,1)} %bitcast.173), kind=kOutput, calls=%fused_computation.1 | convolution fusion | flops 204472320 | bytes 26746880 | tf_op jit(solution)/shard_map/kn,snqb->skqb/dot_general | solution.py:30
  92.3 2.9 %add_convert_fusion.1 = (bf16[3,64,32,256]{3,1,2,0:T(8,128)(2,1)S(1)}, bf16[3,64,32,256]{3,1,2,0:T(8,128)(2,1)}) fusion(f32[3,128,32,256]{3,1,2,0:T(8,128)S(1)} %add_bitcast_fusion, f32[64,32]{0,1:T(8,128)S(1)} %copy-done.16, f32[64,32]{0,1:T(8,128)S(1)} %copy-done.17), kind=kLoop, calls=%fused_computation.18 | loop fusion | flops 12582912 | bytes 18890752 | tf_op jit(solution)/shard_map/convert.16
  95.1 2.4 pad_maximum_fusion
  97.6 9.5 %fusion.12 = f32[3,64,64,256]{3,2,1,0:T(8,128)} fusion(bf16[64,64,1,1]{1,0,3,2:T(8,128)(2,1)S(1)} %copy-done.19, bf16[3,64,64,256]{3,1,2,0:T(8,128)(2,1)S(1)} %pad_maximum_fusion), kind=kOutput, calls=%fused_computation.19 | convolution fusion | flops 402653184 | bytes 18882560 | tf_op jit(solution)/shard_map/ab,skbc->skac/dot_general | solution.py:27
  107.0 9.7 %slice_bitcast_fusion.1 = (f32[64,64,256]{2,1,0:T(8,128)}, f32[64,64,256]{2,1,0:T(8,128)}, f32[64,64,256]{2,1,0:T(8,128)}) fusion(f32[3,64,64,256]{3,2,1,0:T(8,128)} %fusion.12), kind=kLoop, calls=%fused_computation.21 | loop fusion | bytes 25165824 | tf_op jit(solution)/shard_map/squeeze | solution.py:91
  116.7 4.8 %add_convert_fusion.3 = (bf16[64,32,256]{2,1,0:T(8,128)(2,1)S(1)}, bf16[64,32,256]{2,1,0:T(8,128)(2,1)S(1)}) fusion(f32[64,64,256]{2,1,0:T(8,128)} %get-tuple-element.62, f32[64,64,256]{2,1,0:T(8,128)} %get-tuple-element.61), kind=kLoop, calls=%fused_computation.30 | loop fusion | flops 4194304 | bytes 10485760 | tf_op jit(solution)/shard_map/convert.11
  122.6 3.6 %subtract_convert_fusion.4 = (bf16[64,32,256]{2,1,0:T(8,128)(2,1)S(1)}, bf16[64,32,256]{2,1,0:T(8,128)(2,1)S(1)}, bf16[64,32,256]{2,1,0:T(8,128)(2,1)S(1)}, bf16[64,32,256]{2,1,0:T(8,128)(2,1)S(1)}) fusion(f32[64,64,256]{2,1,0:T(8,128)S(1)} %copy-done, f32[64,64,256]{2,1,0:T(8,128)} %get-tuple-element.63, f32[64,64,256]{2,1,0:T(8,128)S(1)} %copy-done.1), kind=kLoop, calls=%fused_computation.32 | loop fusion | flops 8388608 | bytes 16777216 | tf_op jit(solution)/shard_map/convert.14
  127.3 5.6 %fusion = f32[3,64,256,64]{2,3,1,0:T(8,128)} fusion(bf16[64,64,1,1]{1,0,3,2:T(8,128)(2,1)S(1)} %copy-done.18, bf16[1,64,64,256]{3,2,1,0:T(8,128)(2,1)S(1)} %maximum_bitcast_fusion.2, bf16[1,64,64,256]{3,2,1,0:T(8,128)(2,1)S(1)} %maximum_bitcast_fusion.1, bf16[1,64,64,256]{3,2,1,0:T(8,128)(2,1)S(1)} %maximum_bitcast_fusion), kind=kOutput, calls=%fused_computation.3 | convolution fusion | flops 421527552 | bytes 18882560 | tf_op jit(solution)/shard_map/ab,skbc->skac/dot_general | solution.py:27
  132.9 16.3 %copy.140 = f32[3,64,256,64]{2,1,3,0:T(8,128)} copy(f32[3,64,256,64]{2,3,1,0:T(8,128)} %fusion) | data formatting | bytes 25165824 | tf_op jit(solution)/shard_map/ab,skbc->skac/dot_general | solution.py:27
  149.2 5.5 %subtract_convert_fusion = (bf16[3,64,32,256]{3,1,2,0:T(8,128)(2,1)S(1)}, bf16[3,64,32,256]{3,1,2,0:T(8,128)(2,1)S(1)}) fusion(f32[3,64,64,256]{3,1,2,0:T(8,128)} %bitcast.171, f32[64,32]{0,1:T(8,128)S(1)} %copy-done.16, f32[64,32]{0,1:T(8,128)S(1)} %copy-done.17), kind=kLoop, calls=%fused_computation.16 | loop fusion | flops 12582912 | bytes 18890752 | tf_op jit(solution)/shard_map/convert.2
  162.6 4.3 %all-to-all-start.1 = ((bf16[3,8,130,256]{3,2,0,1:T(8,128)(2,1)}), bf16[3,8,130,256]{3,2,0,1:T(8,128)(2,1)}, u32[]{:S(2)}, u32[]{:S(2)}) async-start(bf16[3,8,130,256]{3,2,0,1:T(8,128)(2,1)} %fusion.73), calls=%async_computation.1 | async-start | bytes 3342336 | tf_op jit(solution)/shard_map/all_to_all | solution.py:174
  168.6 36.4 %all-to-all-done.1 = bf16[3,8,130,256]{3,2,0,1:T(8,128)(2,1)} async-done(((bf16[3,8,130,256]{3,2,0,1:T(8,128)(2,1)}), bf16[3,8,130,256]{3,2,0,1:T(8,128)(2,1)}, u32[]{:S(2)}, u32[]{:S(2)}) %all-to-all-start.1) | async-done | bytes 1597472 | tf_op jit(solution)/shard_map/all_to_all | solution.py:174
  220.3 3.6 %collective-permute-done.4 = f32[10,2048]{1,0:T(8,128)S(1)} collective-permute-done((f32[10,2048]{1,0:T(8,128)S(1)}, f32[10,2048]{1,0:T(8,128)S(1)}, u32[]{:S(2)}, u32[]{:S(2)}) %collective-permute-start.4) | collective-permute-done | bytes 81952 | tf_op jit(solution)/shard_map/ppermute | solution.py:103
  224.0 5.0 %collective-permute-done.5 = f32[10,2048]{1,0:T(8,128)S(1)} collective-permute-done((f32[10,2048]{1,0:T(8,128)S(1)}, f32[10,2048]{1,0:T(8,128)S(1)}, u32[]{:S(2)}, u32[]{:S(2)}) %collective-permute-start.5) | collective-permute-done | bytes 81952 | tf_op jit(solution)/shard_map/ppermute | solution.py:103
  229.1 3.0 %copy.107 = f32[3,1,130,8,256]{4,3,2,0,1:T(8,128)S(1)} copy(f32[3,1,130,8,256]{4,2,0,3,1:T(8,128)} %copy-done.2) | data formatting | bytes 6389760 | tf_op jit(solution)/shard_map/convert_element_type | solution.py:175
  232.1 2.4 convert_element_type.102
  240.0 13.4 %collective-permute-done.8 = f32[10,2048]{1,0:T(8,128)S(1)} collective-permute-done((f32[10,2048]{1,0:T(8,128)S(1)}, f32[10,2048]{1,0:T(8,128)S(1)}, u32[]{:S(2)}, u32[]{:S(2)}) %collective-permute-start.8) | collective-permute-done | bytes 81952 | tf_op jit(solution)/shard_map/ppermute | solution.py:103
  (141 shorter events, 51.1 us)
Async XLA Ops:
  0.6 15.5 %copy-start.13 = (bf16[1,128,2048]{2,1,0:T(8,128)(2,1)S(1)}, bf16[1,128,2048]{2,1,0:T(8,128)(2,1)}, u32[]{:S(2)}) copy-start(bf16[1,128,2048]{2,1,0:T(8,128)(2,1)} %param.18) | copy-start | bytes 1572868
  3.1 9.8 %collective-permute-start = (bf16[3,2,2048]{2,1,0:T(2,128)(2,1)S(1)}, bf16[3,2,2048]{2,1,0:T(2,128)(2,1)S(1)}, u32[]{:S(2)}, u32[]{:S(2)}) collective-permute-start(bf16[3,2,2048]{2,1,0:T(2,128)(2,1)S(1)} %pad_maximum_fusion.6), channel_id=1, source_target_pairs={{0,1},{1,2},{2,3},{3,4},{4,5},{5,6},{6,7},{8,9},{9,10},{10,11},{11... | collective-permute-start | bytes 73736 | tf_op jit(solution)/shard_map/ppermute | solution.py:14
  9.0 5.8 %collective-permute-start.1 = (bf16[4,2,2048]{2,0,1:T(4,128)(2,1)S(1)}, bf16[4,2,2048]{2,0,1:T(4,128)(2,1)S(1)}, u32[]{:S(2)}, u32[]{:S(2)}) collective-permute-start(bf16[4,2,2048]{2,0,1:T(4,128)(2,1)S(1)} %pad_maximum_fusion.5), channel_id=1, source_target_pairs={{1,0},{2,1},{3,2},{4,3},{5,4},{6,5},{7,6},{9,8},{10,9},{11,10},{12... | collective-permute-start | bytes 98312 | tf_op jit(solution)/shard_map/ppermute | solution.py:14
  16.3 2.4 copy-start.14
  18.7 3.3 %copy-start.3 = (bf16[130,2048]{1,0:T(8,128)(2,1)}, bf16[130,2048]{1,0:T(8,128)(2,1)S(1)}, u32[]{:S(2)}) copy-start(bf16[130,2048]{1,0:T(8,128)(2,1)S(1)} %get-tuple-element.50) | copy-start | bytes 1597444
  19.9 2.9 %copy-start.15 = (bf16[128,2048]{1,0:T(8,128)(2,1)S(1)}, bf16[128,2048]{1,0:T(8,128)(2,1)}, u32[]{:S(2)}) copy-start(bf16[128,2048]{1,0:T(8,128)(2,1)} %param.21) | copy-start | bytes 1572868
  82.8 2.6 %copy-start.21 = (bf16[128,32,1,1]{0,1,3,2:T(8,128)(2,1)S(1)}, bf16[128,32,1,1]{0,1,3,2:T(8,128)(2,1)}, u32[]{:S(2)}) copy-start(bf16[128,32,1,1]{0,1,3,2:T(8,128)(2,1)} %constant.91) | copy-start | bytes 24580
  85.4 3.3 %copy-start.22 = (bf16[128,32,1,1]{0,1,3,2:T(8,128)(2,1)S(1)}, bf16[128,32,1,1]{0,1,3,2:T(8,128)(2,1)}, u32[]{:S(2)}) copy-start(bf16[128,32,1,1]{0,1,3,2:T(8,128)(2,1)} %constant.92) | copy-start | bytes 24580
  88.7 3.6 %copy-start.16 = (f32[64,32]{0,1:T(8,128)S(1)}, f32[64,32]{0,1:T(8,128)}, u32[]{:S(2)}) copy-start(f32[64,32]{0,1:T(8,128)} %constant.80.clone) | copy-start | bytes 24580
  88.7 3.6 %copy-start.17 = (f32[64,32]{0,1:T(8,128)S(1)}, f32[64,32]{0,1:T(8,128)}, u32[]{:S(2)}) copy-start(f32[64,32]{0,1:T(8,128)} %constant.79.clone) | copy-start | bytes 24580
  95.1 2.5 copy-start.19
  116.7 4.8 %copy-start = (f32[64,64,256]{2,1,0:T(8,128)S(1)}, f32[64,64,256]{2,1,0:T(8,128)}, u32[]{:S(2)}) copy-start(f32[64,64,256]{2,1,0:T(8,128)} %get-tuple-element.61) | copy-start | bytes 12582916
  116.7 5.9 %copy-start.1 = (f32[64,64,256]{2,1,0:T(8,128)S(1)}, f32[64,64,256]{2,1,0:T(8,128)}, u32[]{:S(2)}) copy-start(f32[64,64,256]{2,1,0:T(8,128)} %get-tuple-element.62) | copy-start | bytes 12582916
  149.2 5.5 %copy-start.23 = (bf16[32,128,1,1]{1,0,3,2:T(8,128)(2,1)S(1)}, bf16[32,128,1,1]{1,0,3,2:T(8,128)(2,1)}, u32[]{:S(2)}) copy-start(bf16[32,128,1,1]{1,0,3,2:T(8,128)(2,1)} %constant.95) | copy-start | bytes 24580
  162.6 42.4 %all-to-all-start.1 = ((bf16[3,8,130,256]{3,2,0,1:T(8,128)(2,1)}), bf16[3,8,130,256]{3,2,0,1:T(8,128)(2,1)}, u32[]{:S(2)}, u32[]{:S(2)}) async-start(bf16[3,8,130,256]{3,2,0,1:T(8,128)(2,1)} %fusion.73), calls=%async_computation.1 | async-start | bytes 3342336 | tf_op jit(solution)/shard_map/all_to_all | solution.py:174
  218.9 5.0 %collective-permute-start.4 = (f32[10,2048]{1,0:T(8,128)S(1)}, f32[10,2048]{1,0:T(8,128)S(1)}, u32[]{:S(2)}, u32[]{:S(2)}) collective-permute-start(f32[10,2048]{1,0:T(8,128)S(1)} %pad_maximum_fusion.3), channel_id=1, source_target_pairs={{0,1},{1,0},{2,3},{3,2},{4,5},{5,4},{6,7},{7,6},{8,9},{9,8},{10,11... | collective-permute-start | bytes 245768 | tf_op jit(solution)/shard_map/ppermute | solution.py:103
  223.9 5.0 %collective-permute-start.5 = (f32[10,2048]{1,0:T(8,128)S(1)}, f32[10,2048]{1,0:T(8,128)S(1)}, u32[]{:S(2)}, u32[]{:S(2)}) collective-permute-start(f32[10,2048]{1,0:T(8,128)S(1)} %fusion.101), channel_id=1, source_target_pairs={{0,2},{1,3},{2,0},{3,1},{4,6},{5,7},{6,4},{7,5},{8,10},{9,11},{10,... | collective-permute-start | bytes 245768 | tf_op jit(solution)/shard_map/ppermute | solution.py:103
  229.0 7.1 %collective-permute-start.6 = (f32[10,2048]{1,0:T(8,128)S(1)}, f32[10,2048]{1,0:T(8,128)S(1)}, u32[]{:S(2)}, u32[]{:S(2)}) collective-permute-start(f32[10,2048]{1,0:T(8,128)S(1)} %add.140), channel_id=1, source_target_pairs={{0,4},{1,5},{2,6},{3,7},{4,0},{5,1},{6,2},{7,3},{8,12},{9,13},{10,... | collective-permute-start | bytes 245768 | tf_op jit(solution)/shard_map/ppermute | solution.py:103
  236.1 3.0 %copy-start.7 = (f32[130,2048]{1,0:T(8,128)S(1)}, f32[130,2048]{1,0:T(8,128)}, u32[]{:S(2)}) copy-start(f32[130,2048]{1,0:T(8,128)} %get-tuple-element.102) | copy-start | bytes 3194884
  236.1 3.0 %copy-start.8 = (f32[130,2048]{1,0:T(8,128)S(1)}, f32[130,2048]{1,0:T(8,128)}, u32[]{:S(2)}) copy-start(f32[130,2048]{1,0:T(8,128)} %get-tuple-element.48) | copy-start | bytes 3194884
  236.1 1.7 collective-permute-start.7
  236.3 17.9 %collective-permute-start.2 = (f32[128,2,512]{0,2,1:T(8,128)S(1)}, f32[128,2,512]{0,2,1:T(8,128)S(1)}, u32[]{:S(2)}, u32[]{:S(2)}) collective-permute-start(f32[128,2,512]{0,2,1:T(8,128)S(1)} %slice_select_fusion.6), channel_id=1, source_target_pairs={{0,16},{8,24},{16,0},{24,8},{1,17},{9,25},{17,1},{25,9},{2,18},{10... | collective-permute-start | bytes 1572872 | tf_op jit(solution)/shard_map/ppermute | solution.py:119
  237.8 15.6 %collective-permute-start.8 = (f32[10,2048]{1,0:T(8,128)S(1)}, f32[10,2048]{1,0:T(8,128)S(1)}, u32[]{:S(2)}, u32[]{:S(2)}) collective-permute-start(f32[10,2048]{1,0:T(8,128)S(1)} %add.142), channel_id=1, source_target_pairs={{0,16},{8,24},{16,0},{24,8},{1,17},{9,25},{17,1},{25,9},{2,18},{10... | collective-permute-start | bytes 245768 | tf_op jit(solution)/shard_map/ppermute | solution.py:103
  254.3 1.6 collective-permute-start.3
  (10 other events, 13.0 us)
